TPU v7x, 128 devices: a whole 4x4x4 slice. The times are simulated.
128 devices in a mesh: bond: 8 (over x, core), op: 16 (over y, z).
Axes of the slice: x: 4, y: 4, z: 4, core: 2. Of those that a mesh axis runs over, the one named last changes fastest.
Arguments:
- wave_slab: bfloat16 [8192, 8192], P('op', 'bond'), may hold values from -6 to 6
- left_blocks: bfloat16 [32, 16, 2, 128, 128], P('op'), may hold values from -0.375 to 0.375
- right_blocks: bfloat16 [32, 64, 2, 128, 128], P('op'), may hold values from -0.0625 to 0.0625
- sector_size: int32 [64], replicated, may hold values from 1 to 128
- left_pairs: int32 [32, 16, 2], P('op'), may hold values from 0 to 63
- right_pairs: int32 [32, 64, 2], P('op'), may hold values from 0 to 63
Outputs:
- applied: float32 [2048, 8192], P('bond', 'op')
All inputs are finite; a program needn't handle non-finite values.
Results may differ from a plain program's by a relative error of at most 0.0029.
Values may be sent and summed in bfloat16 or wider, within the bound.
No kernel may reach another device: no remote copies, remote signals or barrier semaphores. Data moves between devices by JAX's collectives and lax.ppermute only.
A program may use at most 128 MiB of HBM per device.

v0:
```python
import jax
import jax.numpy as jnp
from jax import lax
from jax.sharding import PartitionSpec as P

TILE = 128


def live_mask(sector_size):
    states = jnp.arange(TILE, dtype=jnp.int32)
    return (states[None, :] < sector_size[:, None]).astype(jnp.float32).reshape(-1)


def on_device(wave_slab, left_blocks, right_blocks, sector_size, left_pairs, right_pairs):
    live = live_mask(sector_size)
    local_rows = wave_slab.shape[0]
    strip = wave_slab.shape[1]
    row_live = lax.dynamic_slice_in_dim(live, lax.axis_index("op") * local_rows, local_rows)
    col_live = lax.dynamic_slice_in_dim(live, lax.axis_index("bond") * strip, strip)
    masked = (wave_slab.astype(jnp.float32) * row_live[:, None] * col_live[None, :]).astype(
        jnp.bfloat16
    )
    whole = lax.all_gather(masked, "op", axis=0, tiled=True)
    full_width = whole.shape[0]
    sector_count = full_width // TILE
    sectors = whole.reshape(sector_count, TILE, strip)
    term_count = left_blocks.shape[0]
    middles = []
    for term_idx in range(term_count):
        picked = sectors[left_pairs[term_idx]]
        middle = jnp.einsum(
            "ipxy,ipys->ixs", left_blocks[term_idx], picked, preferred_element_type=jnp.float32
        )
        middles.append(middle.astype(jnp.bfloat16).reshape(-1, strip))
    stacked = jnp.stack(middles, 0)
    bond_count = lax.axis_size("bond")
    slab_rows = stacked.shape[1]
    share_rows = slab_rows // bond_count
    blocked = stacked.reshape(term_count, bond_count, share_rows, strip)
    arrived = lax.all_to_all(blocked, "bond", split_axis=1, concat_axis=3, tiled=True)
    row_count = arrived.shape[2]
    total = jnp.zeros((row_count, sector_count, TILE), jnp.float32)
    for term_idx in range(term_count):
        split_cols = arrived[term_idx, 0].reshape(row_count, sector_count, TILE)
        chosen = split_cols[:, right_pairs[term_idx]]
        total = total + jnp.einsum(
            "rjpy,jpyz->rjz", chosen, right_blocks[term_idx], preferred_element_type=jnp.float32
        )
    partial_value = total.reshape(row_count, full_width)
    summed = lax.psum_scatter(partial_value, "op", scatter_dimension=1, tiled=True)
    out_cols = summed.shape[1]
    out_row_live = lax.dynamic_slice_in_dim(live, lax.axis_index("bond") * share_rows, share_rows)
    out_col_live = lax.dynamic_slice_in_dim(live, lax.axis_index("op") * out_cols, out_cols)
    return summed * out_row_live[:, None] * out_col_live[None, :]


def solution(mesh):
    placed = (
        P("op", "bond"),
        P("op", None, None, None, None),
        P("op", None, None, None, None),
        P(),
        P("op", None, None),
        P("op", None, None),
    )
    return jax.shard_map(
        on_device, mesh=mesh, in_specs=placed, out_specs=P("bond", "op"), check_vma=False
    )
```

profile of v0, /device:TPU:0, one launch (start us, length us, event | category | flops | bytes accessed | tf_op | source)
XLA Modules:
  0.0 447.6 jit_solution(14537597451842649991)
XLA Ops:
  6.5 0.0 all-gather.2.cloned.1.call-start
  6.5 0.7 convert_bitcast_fusion
  7.3 0.1 dynamic_slice.10
  7.4 2.5 multiply_convert_fusion
  9.9 0.0 all-gather.2.cloned.1.call-update
  9.9 0.7 compare_select_fusion.3
  10.6 0.1 copy.25
  10.7 0.1 reshape.143
  10.8 0.1 copy.26
  10.9 0.1 reshape.151
  11.0 112.9 %all-gather.2.cloned.1.call-done = bf16[8192,1024]{1,0:T(8,128)(2,1)} async-done(((bf16[512,1024]{1,0:T(8,128)(2,1)}), bf16[8192,1024]{1,0:T(8,128)(2,1)}) %all-gather.2.cloned.1.call-update) | async-done | bytes 16777232 | tf_op jit(solution)/shard_map/all_gather | solution.py:23
  123.9 0.0 copy-start
  123.9 10.9 %gather_fusion = bf16[32,128,1024]{2,1,0:T(8,128)(2,1)} fusion(bf16[64,128,1024]{2,1,0:T(8,128)(2,1)} %bitcast.83, s32[1024]{0:T(1024)S(1)} %pad_clamp_fusion.3), kind=kCustom, calls=%fused_computation | custom fusion | bytes 16777344 | tf_op jit(solution)/shard_map/gather | solution.py:30
  134.8 0.0 copy-done
  134.8 6.6 %bitcast_convert_fusion.1 = bf16[16,1024,128]{1,2,0:T(8,128)(2,1)} fusion(bf16[16,2,128,1024]{3,2,1,0:T(8,128)(2,1)} %bitcast.76, bf16[2,16,2,128,128]{4,3,2,1,0:T(8,128)(2,1)S(1)} %copy-done), kind=kOutput, calls=%fused_computation.7 | convolution fusion | flops 1075838976 | bytes 13631488 | tf_op jit(solution)/shard_map/ipxy,ipys->ixs/dot_general | solution.py:31
  141.4 6.4 %copy.27 = bf16[1,8,256,1024]{2,3,0,1:T(8,128)(2,1)} copy(bf16[1,8,256,1024]{3,2,1,0:T(8,128)(2,1)} %bitcast.81) | data formatting | bytes 8388608 | tf_op jit(solution)/shard_map/stack | solution.py:35
  147.8 10.8 %gather_fusion.1 = bf16[32,128,1024]{2,1,0:T(8,128)(2,1)} fusion(bf16[64,128,1024]{2,1,0:T(8,128)(2,1)} %bitcast.84, s32[1024]{0:T(1024)S(1)} %pad_clamp_fusion.2), kind=kCustom, calls=%fused_computation.1 | custom fusion | bytes 16777344 | tf_op jit(solution)/shard_map/gather | solution.py:30
  158.6 6.6 %bitcast_convert_fusion = bf16[16,1024,128]{1,2,0:T(8,128)(2,1)} fusion(bf16[16,2,128,1024]{3,2,1,0:T(8,128)(2,1)} %bitcast.75, bf16[2,16,2,128,128]{4,3,2,1,0:T(8,128)(2,1)S(1)} %copy-done), kind=kOutput, calls=%fused_computation.6 | convolution fusion | flops 1075838976 | bytes 13631488 | tf_op jit(solution)/shard_map/ipxy,ipys->ixs/dot_general | solution.py:31
  165.2 6.5 %copy.28 = bf16[1,8,256,1024]{2,3,0,1:T(8,128)(2,1)} copy(bf16[1,8,256,1024]{3,2,1,0:T(8,128)(2,1)} %bitcast.82) | data formatting | bytes 8388608 | tf_op jit(solution)/shard_map/stack | solution.py:35
  171.7 7.5 %pad_maximum_fusion = bf16[2,8,256,1024]{2,3,0,1:T(8,128)(2,1)} fusion(bf16[1,8,256,1024]{2,3,0,1:T(8,128)(2,1)} %copy.28, bf16[1,8,256,1024]{2,3,0,1:T(8,128)(2,1)} %copy.27), kind=kLoop, calls=%fused_computation.4 | loop fusion | flops 4194304 | bytes 16777216 | tf_op jit(solution)/shard_map/stack | solution.py:35
  179.1 0.0 copy-start.1
  179.1 5.2 %all-to-all-start = ((bf16[2,8,256,1024]{2,3,0,1:T(8,128)(2,1)}), bf16[2,8,256,1024]{2,3,0,1:T(8,128)(2,1)}, u32[]{:S(2)}, u32[]{:S(2)}) async-start(bf16[2,8,256,1024]{2,3,0,1:T(8,128)(2,1)} %pad_maximum_fusion), calls=%async_computation | async-start | bytes 16777216 | tf_op jit(solution)/shard_map/all_to_all | solution.py:40
  184.3 0.2 reduce-scatter.2.cloned.1.call-start
  184.5 0.0 copy-done.1
  184.5 0.1 copy.33
  184.6 0.1 reshape.167
  184.8 0.1 copy.30
  184.9 0.1 reshape.159
  185.0 93.8 %all-to-all-done = bf16[2,8,256,1024]{2,3,0,1:T(8,128)(2,1)} async-done(((bf16[2,8,256,1024]{2,3,0,1:T(8,128)(2,1)}), bf16[2,8,256,1024]{2,3,0,1:T(8,128)(2,1)}, u32[]{:S(2)}, u32[]{:S(2)}) %all-to-all-start) | async-done | bytes 8388640 | tf_op jit(solution)/shard_map/all_to_all | solution.py:40
  278.9 7.3 %copy.44 = bf16[2,8,256,1024]{2,3,1,0:T(8,128)(2,1)} copy(bf16[2,8,256,1024]{2,3,0,1:T(8,128)(2,1)} %all-to-all-done) | data formatting | bytes 16777216 | tf_op jit(solution)/shard_map/all_to_all | solution.py:40
  286.2 5.7 %fusion.12 = (bf16[1,1,256,8,1024]{2,4,3,1,0:T(8,128)(2,1)}, bf16[1,1,256,8,1024]{2,4,3,1,0:T(8,128)(2,1)}) fusion(bf16[2,1,256,8,1024]{2,4,3,1,0:T(8,128)(2,1)} %bitcast.79), kind=kLoop, calls=%fused_computation.31 | loop fusion | bytes 16777216 | tf_op jit(solution)/shard_map/slice | solution.py:44
  291.9 6.4 %copy.34 = bf16[256,64,128]{2,0,1:T(8,128)(2,1)} copy(bf16[256,64,128]{0,2,1:T(8,128)(2,1)} %bitcast.86) | data formatting | bytes 8388608 | tf_op jit(solution)/shard_map/reshape;squeeze | solution.py:44
  298.3 6.3 %copy.31 = bf16[256,64,128]{2,0,1:T(8,128)(2,1)} copy(bf16[256,64,128]{0,2,1:T(8,128)(2,1)} %bitcast.85) | data formatting | bytes 8388608 | tf_op jit(solution)/shard_map/reshape;squeeze | solution.py:44
  304.6 8.8 %gather_fusion.3 = bf16[128,256,128]{2,1,0:T(8,128)(2,1)} fusion(bf16[256,64,128]{2,0,1:T(8,128)(2,1)} %copy.34, s32[1024]{0:T(1024)S(1)} %pad_clamp_fusion), kind=kCustom, calls=%fused_computation.3 | custom fusion | bytes 16777728 | tf_op jit(solution)/shard_map/gather | solution.py:45
  313.4 10.7 %fusion = f32[64,256,128,1]{1,2,3,0:T(8,128)} fusion(bf16[256,64,2,128]{3,0,2,1:T(8,128)(2,1)} %bitcast.80, bf16[2,64,2,128,128]{4,3,2,1,0:T(8,128)(2,1)} %param.8), kind=kOutput, calls=%fused_computation.9 | convolution fusion | flops 1073741824 | bytes 20971520 | tf_op jit(solution)/shard_map/rjpy,jpyz->rjz/dot_general | solution.py:46
  324.1 8.8 %gather_fusion.2 = bf16[128,256,128]{2,1,0:T(8,128)(2,1)} fusion(bf16[256,64,128]{2,0,1:T(8,128)(2,1)} %copy.31, s32[1024]{0:T(1024)S(1)} %pad_clamp_fusion.1), kind=kCustom, calls=%fused_computation.2 | custom fusion | bytes 16777728 | tf_op jit(solution)/shard_map/gather | solution.py:45
  332.8 13.2 %bitcast_add_fusion = f32[64,256,128]{1,2,0:T(8,128)} fusion(f32[64,256,128,1]{1,2,3,0:T(8,128)} %fusion, bf16[256,64,2,128]{3,0,2,1:T(8,128)(2,1)} %bitcast.77, bf16[2,64,2,128,128]{4,3,2,1,0:T(8,128)(2,1)} %param.8), kind=kOutput, calls=%fused_computation.5 | convolution fusion | flops 1075838976 | bytes 29360128 | tf_op jit(solution)/shard_map/rjpy,jpyz->rjz/dot_general | solution.py:46
  346.0 8.9 %copy.36 = f32[256,8192]{1,0:T(8,128)} copy(f32[256,8192]{0,1:T(8,128)} %bitcast.78) | data formatting | bytes 16777216 | tf_op jit(solution)/shard_map/reshape | solution.py:49
  354.9 0.0 reduce-scatter.2.cloned.1.call-update
  354.9 0.1 dynamic_slice.12
  355.0 83.9 %reduce-scatter.2.cloned.1.call-done = f32[256,512]{1,0:T(8,128)} async-done(((f32[256,8192]{1,0:T(8,128)}), f32[256,512]{1,0:T(8,128)}) %reduce-scatter.2.cloned.1.call-update) | async-done | bytes 524304 | tf_op jit(solution)/shard_map/reduce_scatter | solution.py:50
  438.9 1.9 multiply_multiply_fusion
  (6 shorter events, 0.0 us)
Async XLA Ops:
  6.5 117.3 %all-gather.2.cloned.1.call-start = ((), (), s32[]{:S(2)}) async-start(), calls=%async_computation.2 | async-start | bytes 17825792 | tf_op jit(solution)/shard_map/all_gather | solution.py:23
  123.9 10.9 %copy-start = (bf16[2,16,2,128,128]{4,3,2,1,0:T(8,128)(2,1)S(1)}, bf16[2,16,2,128,128]{4,3,2,1,0:T(8,128)(2,1)}, u32[]{:S(2)}) copy-start(bf16[2,16,2,128,128]{4,3,2,1,0:T(8,128)(2,1)} %param.7) | copy-start | bytes 6291460
  179.1 5.4 %copy-start.1 = (s32[2,64,2]{1,2,0:T(2,128)S(1)}, s32[2,64,2]{1,2,0:T(2,128)}, u32[]{:S(2)}) copy-start(s32[2,64,2]{1,2,0:T(2,128)} %param.11) | copy-start | bytes 3076
  179.1 99.8 %all-to-all-start = ((bf16[2,8,256,1024]{2,3,0,1:T(8,128)(2,1)}), bf16[2,8,256,1024]{2,3,0,1:T(8,128)(2,1)}, u32[]{:S(2)}, u32[]{:S(2)}) async-start(bf16[2,8,256,1024]{2,3,0,1:T(8,128)(2,1)} %pad_maximum_fusion), calls=%async_computation | async-start | bytes 16777216 | tf_op jit(solution)/shard_map/all_to_all | solution.py:40
  184.3 254.6 %reduce-scatter.2.cloned.1.call-start = ((), (), s32[]{:S(2)}) async-start(), calls=%async_computation.3 | async-start | bytes 8912896 | tf_op jit(solution)/shard_map/reduce_scatter | solution.py:50
Sparse Core Ops, SparseCore 0:
  10.0 113.8 all-gather.1
  355.0 83.7 reduce-scatter.1
where the time goes:
time: 449 us; the launch traced here: 448 us
  waiting for transfers between devices  291 us (65%)
  local copies, waits for them, and re-layouts  87.8 us (20%)
  matrix products  37 us (8%)
  between operations  13.5 us (3%)
  other arithmetic  13.4 us (3%)
  starting transfers between devices  5.4 us (1%)
    all_gather x1, waiting for transfers between devices, on_device(): whole = lax.all_gather(masked, 'op', axis=0, tiled=True)  113 us
    all_to_all x1, waiting for transfers between devices, on_device(): lax.all_to_all(blocked, 'bond', split_axis=1, concat_axis=3, tiled=True)  93.8 us
    reduce_scatter x1, waiting for transfers between devices, on_device(): lax.psum_scatter(partial_value, 'op', scatter_dimension=1, tiled=True)  83.9 us
    dot_general x2, matrix products, on_device(): jnp.einsum('rjpy,jpyz->rjz', chosen, right_blocks[term_idx], preferred_el...  23.8 us
    gather x2, local copies, waits for them, and re-layouts, on_device(): picked = sectors[left_pairs[term_idx]]  21.7 us
    gather x2, local copies, waits for them, and re-layouts, on_device(): chosen = split_cols[:, right_pairs[term_idx]]  17.6 us
    dot_general x2, matrix products, on_device(): jnp.einsum('ipxy,ipys->ixs', left_blocks[term_idx], picked, preferred_ele...  13.2 us
    another operation x2, local copies, waits for them, and re-layouts, on_device(): stacked = jnp.stack(middles, 0)  12.9 us
  transfers between devices with their start and end apart: 3, of which 3 were waited for; matrix products, arithmetic and copies ran while one was open for 0% of the time, Pallas kernels for 0%

commit v1 on v0

--- a/solution.py
+++ b/solution.py
@@ -37,7 +37,10 @@
     slab_rows = stacked.shape[1]
     share_rows = slab_rows // bond_count
     blocked = stacked.reshape(term_count, bond_count, share_rows, strip)
-    arrived = lax.all_to_all(blocked, "bond", split_axis=1, concat_axis=3, tiled=True)
+    arrived = jnp.concatenate(
+        lax.all_to_all(jnp.stack(jnp.split(blocked, lax.axis_size("bond"), axis=1)), "bond", 0, 0),
+        axis=3,
+    )
     row_count = arrived.shape[2]
     total = jnp.zeros((row_count, sector_count, TILE), jnp.float32)
     for term_idx in range(term_count):

time: 449 us -> 453 us (level)
    unnamed x0 -> x7, other arithmetic: none -> 8.75 us
    another operation x1, other arithmetic: 7.46 us -> 1.08 us  [on_device(): jnp.stack(jnp.split(blocked, lax.axis_size('bond'), axis=1))]
where the time goes in v1:
time: 453 us; the launch traced here: 452 us
  waiting for transfers between devices  290 us (64%)
  local copies, waits for them, and re-layouts  89.7 us (20%)
  matrix products  37 us (8%)
  other arithmetic  15.7 us (3%)
  between operations  13.5 us (3%)
  starting transfers between devices  5.38 us (1%)
    all_gather x1, waiting for transfers between devices, on_device(): whole = lax.all_gather(masked, 'op', axis=0, tiled=True)  113 us
    all_to_all x1, waiting for transfers between devices, on_device(): lax.all_to_all(jnp.stack(jnp.split(blocked, lax.axis_size('bond'), axis=1...  93.8 us
    reduce_scatter x1, waiting for transfers between devices, on_device(): lax.psum_scatter(partial_value, 'op', scatter_dimension=1, tiled=True)  83.7 us
    dot_general x2, matrix products, on_device(): jnp.einsum('rjpy,jpyz->rjz', chosen, right_blocks[term_idx], preferred_el...  23.8 us
    gather x2, local copies, waits for them, and re-layouts, on_device(): picked = sectors[left_pairs[term_idx]]  21.8 us
    gather x2, local copies, waits for them, and re-layouts, on_device(): chosen = split_cols[:, right_pairs[term_idx]]  17.5 us
    dot_general x2, matrix products, on_device(): jnp.einsum('ipxy,ipys->ixs', left_blocks[term_idx], picked, preferred_ele...  13.2 us
    another operation x2, local copies, waits for them, and re-layouts, on_device(): stacked = jnp.stack(middles, 0)  12.9 us
  transfers between devices with their start and end apart: 3, of which 3 were waited for; matrix products, arithmetic and copies ran while one was open for 0% of the time, Pallas kernels for 0%

profile of v1, /device:TPU:0, one launch (start us, length us, event | category | flops | bytes accessed | tf_op | source)
XLA Modules:
  0.0 451.8 jit_solution(15249644536887594395)
XLA Ops:
  6.5 0.0 all-gather.2.cloned.1.call-start
  6.5 0.7 convert_bitcast_fusion
  7.3 0.1 dynamic_slice.10
  7.4 2.5 multiply_convert_fusion
  9.9 0.0 all-gather.2.cloned.1.call-update
  9.9 0.7 compare_select_fusion.3
  10.6 0.1 copy.39
  10.7 0.1 reshape.148
  10.8 0.1 copy.40
  10.9 0.1 reshape.156
  11.0 112.9 %all-gather.2.cloned.1.call-done = bf16[8192,1024]{1,0:T(8,128)(2,1)} async-done(((bf16[512,1024]{1,0:T(8,128)(2,1)}), bf16[8192,1024]{1,0:T(8,128)(2,1)}) %all-gather.2.cloned.1.call-update) | async-done | bytes 16777232 | tf_op jit(solution)/shard_map/all_gather | solution.py:23
  123.9 11.0 %gather_fusion = bf16[32,128,1024]{2,1,0:T(8,128)(2,1)} fusion(bf16[64,128,1024]{2,1,0:T(8,128)(2,1)} %bitcast.113, s32[1024]{0:T(1024)S(1)} %get-tuple-element.14), kind=kCustom, calls=%fused_computation | custom fusion | bytes 16777344 | tf_op jit(solution)/shard_map/gather | solution.py:30
  134.9 0.0 copy-done.2
  134.9 6.6 %bitcast_convert_fusion.1 = bf16[16,1024,128]{1,2,0:T(8,128)(2,1)} fusion(bf16[16,2,128,1024]{3,2,1,0:T(8,128)(2,1)} %bitcast.106, bf16[2,16,2,128,128]{4,3,2,1,0:T(8,128)(2,1)S(1)} %copy-done.2), kind=kOutput, calls=%fused_computation.20 | convolution fusion | flops 1075838976 | bytes 13631488 | tf_op jit(solution)/shard_map/ipxy,ipys->ixs/dot_general | solution.py:31
  141.5 6.5 %copy.41 = bf16[1,8,256,1024]{2,3,0,1:T(8,128)(2,1)} copy(bf16[1,8,256,1024]{3,2,1,0:T(8,128)(2,1)} %bitcast.111) | data formatting | bytes 8388608 | tf_op jit(solution)/shard_map/stack | solution.py:35
  148.0 10.8 %gather_fusion.1 = bf16[32,128,1024]{2,1,0:T(8,128)(2,1)} fusion(bf16[64,128,1024]{2,1,0:T(8,128)(2,1)} %bitcast.114, s32[1024]{0:T(1024)S(1)} %get-tuple-element.13), kind=kCustom, calls=%fused_computation.1 | custom fusion | bytes 16777344 | tf_op jit(solution)/shard_map/gather | solution.py:30
  158.7 6.6 %bitcast_convert_fusion = bf16[16,1024,128]{1,2,0:T(8,128)(2,1)} fusion(bf16[16,2,128,1024]{3,2,1,0:T(8,128)(2,1)} %bitcast.105, bf16[2,16,2,128,128]{4,3,2,1,0:T(8,128)(2,1)S(1)} %copy-done.2), kind=kOutput, calls=%fused_computation.19 | convolution fusion | flops 1075838976 | bytes 13631488 | tf_op jit(solution)/shard_map/ipxy,ipys->ixs/dot_general | solution.py:31
  165.3 6.4 %copy.42 = bf16[1,8,256,1024]{2,3,0,1:T(8,128)(2,1)} copy(bf16[1,8,256,1024]{3,2,1,0:T(8,128)(2,1)} %bitcast.112) | data formatting | bytes 8388608 | tf_op jit(solution)/shard_map/stack | solution.py:35
  171.8 2.4 bitcast_dynamic-update-slice_fusion.6
  174.2 0.5 copy-done
  174.6 1.3 copy-done.1
  175.9 1.1 bitcast_dynamic-update-slice_fusion.5
  177.0 1.0 bitcast_dynamic-update-slice_fusion.4
  178.0 1.1 bitcast_dynamic-update-slice_fusion.3
  179.1 1.0 bitcast_dynamic-update-slice_fusion.2
  180.1 1.1 bitcast_dynamic-update-slice_fusion.1
  181.2 1.1 bitcast_dynamic-update-slice_fusion
  182.3 1.1 fusion.16
  183.4 5.2 %all-to-all-start = ((bf16[8,2,1,256,1024]{3,4,2,1,0:T(8,128)(2,1)}), bf16[8,2,1,256,1024]{3,4,2,1,0:T(8,128)(2,1)}, u32[]{:S(2)}, u32[]{:S(2)}) async-start(bf16[8,2,1,256,1024]{3,4,2,1,0:T(8,128)(2,1)} %fusion.16), calls=%async_computation | async-start | bytes 16777216 | tf_op jit(solution)/shard_map/all_to_all | solution.py:41
  188.5 0.2 reduce-scatter.2.cloned.1.call-start
  188.8 0.1 copy.51
  188.9 0.1 reshape.164
  189.0 0.1 copy.54
  189.1 0.1 reshape.172
  189.3 93.8 %all-to-all-done = bf16[8,2,1,256,1024]{3,4,2,1,0:T(8,128)(2,1)} async-done(((bf16[8,2,1,256,1024]{3,4,2,1,0:T(8,128)(2,1)}), bf16[8,2,1,256,1024]{3,4,2,1,0:T(8,128)(2,1)}, u32[]{:S(2)}, u32[]{:S(2)}) %all-to-all-start) | async-done | bytes 8388640 | tf_op jit(solution)/shard_map/all_to_all | solution.py:41
  283.1 7.4 %copy.65 = bf16[8,2,1,256,1024]{3,4,0,2,1:T(8,128)(2,1)} copy(bf16[8,2,1,256,1024]{3,4,2,1,0:T(8,128)(2,1)} %all-to-all-done) | data formatting | bytes 16777216 | tf_op jit(solution)/shard_map/all_to_all | solution.py:41
  290.5 5.7 %fusion.21 = (bf16[1,1,256,8,1024]{2,4,3,1,0:T(8,128)(2,1)}, bf16[1,1,256,8,1024]{2,4,3,1,0:T(8,128)(2,1)}) fusion(bf16[2,1,256,8,1024]{2,4,3,1,0:T(8,128)(2,1)} %bitcast.109), kind=kLoop, calls=%fused_computation.61 | loop fusion | bytes 16777216 | tf_op jit(solution)/shard_map/slice | solution.py:47
  296.2 6.4 %copy.55 = bf16[256,64,128]{2,0,1:T(8,128)(2,1)} copy(bf16[256,64,128]{0,2,1:T(8,128)(2,1)} %bitcast.116) | data formatting | bytes 8388608 | tf_op jit(solution)/shard_map/reshape;squeeze | solution.py:47
  302.7 6.4 %copy.52 = bf16[256,64,128]{2,0,1:T(8,128)(2,1)} copy(bf16[256,64,128]{0,2,1:T(8,128)(2,1)} %bitcast.115) | data formatting | bytes 8388608 | tf_op jit(solution)/shard_map/reshape;squeeze | solution.py:47
  309.0 8.7 %gather_fusion.3 = bf16[128,256,128]{2,1,0:T(8,128)(2,1)} fusion(bf16[256,64,128]{2,0,1:T(8,128)(2,1)} %copy.55, s32[1024]{0:T(1024)S(1)} %get-tuple-element.11), kind=kCustom, calls=%fused_computation.3 | custom fusion | bytes 16777728 | tf_op jit(solution)/shard_map/gather | solution.py:48
  317.8 10.7 %fusion = f32[64,256,128,1]{1,2,3,0:T(8,128)} fusion(bf16[256,64,2,128]{3,0,2,1:T(8,128)(2,1)} %bitcast.110, bf16[2,64,2,128,128]{4,3,2,1,0:T(8,128)(2,1)} %param.8), kind=kOutput, calls=%fused_computation.22 | convolution fusion | flops 1073741824 | bytes 20971520 | tf_op jit(solution)/shard_map/rjpy,jpyz->rjz/dot_general | solution.py:49
  328.4 8.7 %gather_fusion.2 = bf16[128,256,128]{2,1,0:T(8,128)(2,1)} fusion(bf16[256,64,128]{2,0,1:T(8,128)(2,1)} %copy.52, s32[1024]{0:T(1024)S(1)} %get-tuple-element.12), kind=kCustom, calls=%fused_computation.2 | custom fusion | bytes 16777728 | tf_op jit(solution)/shard_map/gather | solution.py:48
  337.2 13.2 %bitcast_add_fusion = f32[64,256,128]{1,2,0:T(8,128)} fusion(f32[64,256,128,1]{1,2,3,0:T(8,128)} %fusion, bf16[256,64,2,128]{3,0,2,1:T(8,128)(2,1)} %bitcast.107, bf16[2,64,2,128,128]{4,3,2,1,0:T(8,128)(2,1)} %param.8), kind=kOutput, calls=%fused_computation.18 | convolution fusion | flops 1075838976 | bytes 29360128 | tf_op jit(solution)/shard_map/rjpy,jpyz->rjz/dot_general | solution.py:49
  350.3 8.9 %copy.57 = f32[256,8192]{1,0:T(8,128)} copy(f32[256,8192]{0,1:T(8,128)} %bitcast.108) | data formatting | bytes 16777216 | tf_op jit(solution)/shard_map/reshape | solution.py:52
  359.2 0.0 reduce-scatter.2.cloned.1.call-update
  359.3 0.1 dynamic_slice.12
  359.3 83.7 %reduce-scatter.2.cloned.1.call-done = f32[256,512]{1,0:T(8,128)} async-done(((f32[256,8192]{1,0:T(8,128)}), f32[256,512]{1,0:T(8,128)}) %reduce-scatter.2.cloned.1.call-update) | async-done | bytes 524304 | tf_op jit(solution)/shard_map/reduce_scatter | solution.py:53
  443.0 1.9 multiply_multiply_fusion
  (9 shorter events, 0.0 us)
Async XLA Ops:
  6.5 117.3 %all-gather.2.cloned.1.call-start = ((), (), s32[]{:S(2)}) async-start(), calls=%async_computation.2 | async-start | bytes 17825792 | tf_op jit(solution)/shard_map/all_gather | solution.py:23
  123.9 11.0 %copy-start.2 = (bf16[2,16,2,128,128]{4,3,2,1,0:T(8,128)(2,1)S(1)}, bf16[2,16,2,128,128]{4,3,2,1,0:T(8,128)(2,1)}, u32[]{:S(2)}) copy-start(bf16[2,16,2,128,128]{4,3,2,1,0:T(8,128)(2,1)} %param.7) | copy-start | bytes 6291460
  171.8 2.9 copy-start
  171.8 4.2 copy-start.1
  183.4 5.4 %copy-start.3 = (s32[2,64,2]{1,2,0:T(2,128)S(1)}, s32[2,64,2]{1,2,0:T(2,128)}, u32[]{:S(2)}) copy-start(s32[2,64,2]{1,2,0:T(2,128)} %param.11) | copy-start | bytes 3076
  183.4 99.7 %all-to-all-start = ((bf16[8,2,1,256,1024]{3,4,2,1,0:T(8,128)(2,1)}), bf16[8,2,1,256,1024]{3,4,2,1,0:T(8,128)(2,1)}, u32[]{:S(2)}, u32[]{:S(2)}) async-start(bf16[8,2,1,256,1024]{3,4,2,1,0:T(8,128)(2,1)} %fusion.16), calls=%async_computation | async-start | bytes 16777216 | tf_op jit(solution)/shard_map/all_to_all | solution.py:41
  188.5 254.5 %reduce-scatter.2.cloned.1.call-start = ((), (), s32[]{:S(2)}) async-start(), calls=%async_computation.3 | async-start | bytes 8912896 | tf_op jit(solution)/shard_map/reduce_scatter | solution.py:53
Sparse Core Ops, SparseCore 0:
  10.0 113.8 all-gather.1
  359.4 83.6 reduce-scatter.1
